TPU v7x, 32 devices: a whole 2x2x4 slice. The times are simulated.
32 devices in a mesh: text: 4 (over z), det: 8 (over y, x, core).
Axes of the slice: x: 2, y: 2, z: 4, core: 2. Of those that a mesh axis runs over, the one named last changes fastest.
Arguments:
- prompt_embeds: bfloat16 [64, 16, 2048], P('text'), may hold values from -6 to 6
- prompt_len: int32 [64], P('text'), may hold values from 1 to 16
- norm_gain: float32 [2048], replicated, may hold values from 0.5 to 1.5
- w_up: bfloat16 [2048, 8192], P(None, 'det'), may hold values from -0.125 to 0.125
- w_down: bfloat16 [8192, 2048], P('det'), may hold values from -0.0625 to 0.0625
- final_gain: float32 [2048], replicated, may hold values from 0.25 to 1.75
- w_proj: bfloat16 [2048, 256], P('det'), may hold values from -0.125 to 0.125
- queries: bfloat16 [32, 1100, 256], P(('text', 'det')), may hold values from -6 to 6
- assign: int32 [32, 1100], P(('text', 'det')), may hold values from 0 to 127
- valid: int32 [32, 64], P(('text', 'det')), may hold values 0 or 1
Outputs:
- grad_up: float32 [2048, 8192], P('text', 'det')
- grad_down: float32 [8192, 2048], P('det', 'text')
- grad_proj: float32 [2048, 256], P('det')
- grad_queries: float32 [32, 1100, 256], P(('text', 'det'))
Inputs may be any that keep to these rules, and one draw needn't show every extreme that they name: `prompt_len`: every prompt uses at least its first token. `assign`: A value of 64 or more means the query has no concept.
All inputs are finite; a program needn't handle non-finite values. No bound on the sum of `valid` on one device may be relied on, other than what follows from the above.
Results may differ from a plain program's by a relative error of at most 0.025.
Values may be sent and summed in bfloat16 or wider, within the bound.
No kernel may reach another device: no remote copies, remote signals or barrier semaphores. Data moves between devices by JAX's collectives and lax.ppermute only.
A program may use at most 64 MiB of HBM per device.

v0:
```python
import jax
import jax.numpy as jnp
from jax import lax
from jax.sharding import PartitionSpec as P

EPS = 1e-05
ALPHA = 0.25
LOGIT_BIAS = -2.0


def gelu_fn(values):
    return jax.nn.gelu(values, approximate=True)


def focal_total(scores, target, weight):
    log_pos = jax.nn.log_sigmoid(scores)
    log_neg = jax.nn.log_sigmoid(-scores)
    probab = jax.nn.sigmoid(scores)
    pos_term = -ALPHA * target * (1.0 - probab) ** 2 * log_pos
    neg_term = -(1.0 - ALPHA) * (1.0 - target) * probab**2 * log_neg
    return jnp.sum(weight * (pos_term + neg_term))


def body(
    prompt_embeds, prompt_len, norm_gain, w_up, w_down, final_gain, w_proj, queries, assign, valid
):
    per_group, prompt, model_width = prompt_embeds.shape
    tok_rows = per_group * prompt
    det_size = lax.axis_size("det")
    share = model_width // det_size
    offset = lax.axis_index("det") * share
    tokens = prompt_embeds.reshape(tok_rows, model_width).astype(jnp.float32)
    row_mean = jnp.mean(tokens, axis=1, keepdims=True)
    centred = tokens - row_mean
    variance = jnp.mean(centred * centred, axis=1, keepdims=True)
    normed = (centred * lax.rsqrt(variance + EPS) * norm_gain).astype(jnp.bfloat16)
    pre_act = jnp.dot(normed, w_up, preferred_element_type=jnp.float32)
    hidden_act, act_back = jax.vjp(gelu_fn, pre_act)
    hidden = hidden_act.astype(jnp.bfloat16)
    partial_out = jnp.dot(hidden, w_down, preferred_element_type=jnp.float32)
    position = lax.broadcasted_iota(jnp.int32, (per_group, prompt), 1)
    lengths = prompt_len.astype(jnp.float32)
    pool_weight = (position < prompt_len[:, None]).astype(jnp.float32) / lengths[:, None]
    layer_out = tokens + lax.psum(partial_out.astype(jnp.bfloat16), "det").astype(jnp.float32)
    out_mean = jnp.mean(layer_out, axis=1, keepdims=True)
    out_centred = layer_out - out_mean
    out_var = jnp.mean(out_centred * out_centred, axis=1, keepdims=True)
    inv_scale = lax.rsqrt(out_var + EPS)
    out_hat = out_centred * inv_scale
    final = out_hat * final_gain
    pooled_full = jnp.sum(
        final.reshape(per_group, prompt, model_width) * pool_weight[:, :, None], axis=1
    )
    pooled_share = lax.dynamic_slice_in_dim(pooled_full, offset, share, 1)
    pooled_low = pooled_share.astype(jnp.bfloat16)
    feat_part = jnp.dot(pooled_low, w_proj, preferred_element_type=jnp.float32)
    concept_feat = lax.psum(feat_part, "det").astype(jnp.bfloat16)
    all_feat = lax.all_gather(concept_feat, "text", axis=0, tiled=True)
    concept_count = all_feat.shape[0]
    img_count, query_count, query_width = queries.shape
    query_rows = img_count * query_count
    flat_queries = queries.reshape(query_rows, query_width)
    score_scale = query_width ** (-0.5)
    scores = (
        lax.dot_general(
            flat_queries, all_feat, (((1,), (1,)), ((), ())), preferred_element_type=jnp.float32
        )
        * score_scale
        + LOGIT_BIAS
    )
    column = lax.broadcasted_iota(jnp.int32, (img_count, query_count, concept_count), 2)
    target = (assign[:, :, None] == column).astype(jnp.float32).reshape(query_rows, concept_count)
    weight = jnp.broadcast_to(
        valid[:, None, :].astype(jnp.float32), (img_count, query_count, concept_count)
    ).reshape(query_rows, concept_count)
    score_grad = jax.grad(focal_total)(scores, target, weight).astype(jnp.bfloat16)
    query_grad = jnp.dot(score_grad, all_feat, preferred_element_type=jnp.float32) * score_scale
    images = img_count * lax.axis_size("text") * det_size
    feat_terms = lax.dot_general(
        score_grad, flat_queries, (((0,), (0,)), ((), ())), preferred_element_type=jnp.float32
    ) * (score_scale / images)
    feat_owned = lax.psum_scatter(
        feat_terms.astype(jnp.bfloat16), "text", scatter_dimension=0, tiled=True
    ).astype(jnp.float32)
    feat_grad = lax.psum(feat_owned, "det")
    proj_part = jnp.dot(
        pooled_low.astype(jnp.float32).T, feat_grad, precision=lax.Precision.HIGHEST
    )
    proj_grad = lax.psum(proj_part.astype(jnp.bfloat16), "text").astype(jnp.float32)
    pooled_share_grad = jnp.dot(
        feat_grad, w_proj.astype(jnp.float32).T, precision=lax.Precision.HIGHEST
    )
    pooled_whole_grad = lax.all_gather(pooled_share_grad, "det", axis=1, tiled=True)
    final_grad = (pooled_whole_grad[:, None, :] * pool_weight[:, :, None]).reshape(
        tok_rows, model_width
    )
    hat_grad = final_grad * final_gain
    mean_first = jnp.mean(hat_grad, axis=1, keepdims=True)
    mean_second = jnp.mean(hat_grad * out_hat, axis=1, keepdims=True)
    out_grad = ((hat_grad - mean_first - out_hat * mean_second) * inv_scale).astype(jnp.bfloat16)
    down_terms = lax.dot_general(
        hidden, out_grad, (((0,), (0,)), ((), ())), preferred_element_type=jnp.float32
    )
    down_grad = lax.psum_scatter(
        down_terms.astype(jnp.bfloat16), "text", scatter_dimension=1, tiled=True
    ).astype(jnp.float32)
    hidden_grad = lax.dot_general(
        out_grad, w_down, (((1,), (1,)), ((), ())), preferred_element_type=jnp.float32
    )
    pre_grad = act_back(hidden_grad)[0].astype(jnp.bfloat16)
    up_terms = lax.dot_general(
        normed, pre_grad, (((0,), (0,)), ((), ())), preferred_element_type=jnp.float32
    )
    up_grad = lax.psum_scatter(
        up_terms.astype(jnp.bfloat16), "text", scatter_dimension=0, tiled=True
    ).astype(jnp.float32)
    return (up_grad, down_grad, proj_grad, query_grad.reshape(img_count, query_count, query_width))


def solution(mesh):
    return jax.shard_map(
        body,
        mesh=mesh,
        in_specs=(
            P("text", None, None),
            P("text"),
            P(),
            P(None, "det"),
            P("det", None),
            P(),
            P("det", None),
            P(("text", "det"), None, None),
            P(("text", "det"), None),
            P(("text", "det"), None),
        ),
        out_specs=(
            P("text", "det"),
            P("det", "text"),
            P("det", None),
            P(("text", "det"), None, None),
        ),
        check_vma=False,
    )
```

profile of v0, /device:TPU:0, one launch (start us, length us, event | category | flops | bytes accessed | tf_op | source)
XLA Modules:
  0.0 372.0 jit_solution(2198379709322240465)
XLA Ops:
  7.2 0.0 all-reduce.3.cloned.1.call-start
  7.2 1.5 convert_reduce_fusion
  8.8 1.6 fusion.11
  10.4 0.1 div.42
  10.5 0.1 rsqrt.20
  10.6 0.4 fusion.14
  11.0 1.0 copy-done.6
  12.0 3.6 fusion.73
  15.6 1.0 copy-done.4
  16.6 2.3 convolution_convert_fusion.2
  19.0 0.0 all-reduce.3.cloned.1.call-update
  19.0 0.0 reduce-scatter.4.cloned.1.call-start
  19.1 0.1 convert_divide_fusion
  19.2 59.4 %all-reduce.3.cloned.1.call-done = bf16[256,2048]{1,0:T(8,128)(2,1)} async-done(((bf16[256,2048]{1,0:T(8,128)(2,1)}), bf16[256,2048]{1,0:T(8,128)(2,1)}) %all-reduce.3.cloned.1.call-update) | async-done | bytes 1048592 | tf_op jit(solution)/shard_map/psum | solution.py:44
  78.5 1.7 fusion.16
  80.3 0.5 multiply_reduce_fusion.2
  80.8 1.2 multiply_reduce_fusion.1
  82.0 0.1 fusion.62
  82.1 22.3 %psum.29 = bf16[16,256]{1,0:T(8,128)(2,1)S(1)} all-reduce(f32[16,256]{1,0:T(8,128)S(1)} %fusion.62), channel_id=1, replica_groups=mesh['text'=4,'det'=8] {'det'}, use_global_device_ids=true, to_apply=%region_6.0 | all-reduce | flops 4096 | bytes 24576 | tf_op jit(solution)/shard_map/psum | solution.py:57
  104.4 13.1 %all_gather.6 = bf16[64,256]{1,0:T(8,128)(2,1)S(1)} all-gather(bf16[16,256]{1,0:T(8,128)(2,1)S(1)} %psum.29), channel_id=1, replica_groups=mesh['text'=4,'det'=8] {'text'}, dimensions={0}, use_global_device_ids=true | all-gather | bytes 40960 | tf_op jit(solution)/shard_map/all_gather | solution.py:58
  117.5 1.0 fusion.42
  118.6 0.8 fusion.19
  119.5 0.0 all-reduce.5.cloned.1.call-start
  119.5 0.1 div.49
  119.6 18.4 %reduce-scatter.4.cloned.1.call-done = bf16[16,256]{1,0:T(8,128)(2,1)} async-done(((bf16[64,256]{1,0:T(8,128)(2,1)}), bf16[16,256]{1,0:T(8,128)(2,1)}) %reduce-scatter.4.cloned.1.call-update) | async-done | bytes 8208 | tf_op jit(solution)/shard_map/reduce_scatter | solution.py:82
  138.0 22.9 %psum.30 = f32[16,256]{1,0:T(8,128)S(1)} all-reduce(bf16[16,256]{1,0:T(8,128)(2,1)} %reduce-scatter.4.cloned.1.call-done), channel_id=1, replica_groups=mesh['text'=4,'det'=8] {'det'}, use_global_device_ids=true, to_apply=%region_8.10 | all-reduce | flops 4096 | bytes 24576 | tf_op jit(solution)/shard_map/psum | solution.py:85
  160.8 0.2 fusion.74
  161.0 1.0 convolution_convert_fusion.3
  162.1 9.2 %all_gather.7 = f32[16,2048]{1,0:T(8,128)S(1)} all-gather(f32[16,256]{1,0:T(8,128)S(1)} %fusion.74), channel_id=1, replica_groups=mesh['text'=4,'det'=8] {'det'}, dimensions={1}, use_global_device_ids=true | all-gather | bytes 147456 | tf_op jit(solution)/shard_map/all_gather | solution.py:93
  171.3 0.3 multiply_reduce_fusion
  171.6 0.8 fusion.9
  172.4 0.1 div.51
  172.5 0.0 all-reduce.5.cloned.1.call-update
  172.5 0.2 reduce-scatter.6.cloned.1.call-start
  172.7 1.9 fusion.8
  174.6 7.9 %convolution_convert_fusion.1 = bf16[2048,1024]{1,0:T(8,128)(2,1)} fusion(bf16[256,2048]{1,0:T(8,128)(2,1)} %copy-done.6, f32[256,1024]{1,0:T(8,128)} %copy-done.4, bf16[256,2048]{1,0:T(8,128)(2,1)} %fusion.8, bf16[1024,2048]{1,0:T(8,128)(2,1)} %param.15), kind=kOutput, calls=%fused_computation.1 | convolution fusion | flops 2154823680 | bytes 11534336 | tf_op jit(solution)/shard_map/dot_general | solution.py:111
  182.6 0.0 reduce-scatter.8.cloned.1.call-start
  182.6 1.2 copy-done.3
  183.8 0.3 copy-done.5
  184.1 3.5 convolution_convert_fusion
  187.6 0.3 fusion
  187.9 5.7 %copy.14 = f32[1,1100,256]{2,0,1:T(1,128)} copy(f32[1,1100,256]{2,1,0:T(8,128)S(1)} %fusion) | data formatting | bytes 2252800
  193.7 10.8 %all-reduce.5.cloned.1.call-done = bf16[256,256]{1,0:T(8,128)(2,1)} async-done(((bf16[256,256]{1,0:T(8,128)(2,1)}), bf16[256,256]{1,0:T(8,128)(2,1)}) %all-reduce.5.cloned.1.call-update) | async-done | bytes 131088 | tf_op jit(solution)/shard_map/psum | solution.py:89
  204.5 1.6 convert_element_type.116
  206.1 77.0 %reduce-scatter.6.cloned.1.call-done = bf16[512,1024]{1,0:T(8,128)(2,1)} async-done(((bf16[2048,1024]{1,0:T(8,128)(2,1)}), bf16[512,1024]{1,0:T(8,128)(2,1)}) %reduce-scatter.6.cloned.1.call-update) | async-done | bytes 1048592 | tf_op jit(solution)/shard_map/reduce_scatter | solution.py:114
  283.2 2.8 convert_element_type.112
  286.0 76.7 %reduce-scatter.8.cloned.1.call-done = bf16[1024,512]{1,0:T(8,128)(2,1)} async-done(((bf16[1024,2048]{1,0:T(8,128)(2,1)}), bf16[1024,512]{1,0:T(8,128)(2,1)}) %reduce-scatter.8.cloned.1.call-update) | async-done | bytes 1048592 | tf_op jit(solution)/shard_map/reduce_scatter | solution.py:104
  362.6 2.8 convert_element_type.114
  (36 shorter events, 0.2 us)
Async XLA Ops:
  7.2 110.4 %copy-start = (bf16[1,1100,256]{2,1,0:T(8,128)(2,1)S(1)}, bf16[1,1100,256]{2,1,0:T(8,128)(2,1)}, u32[]{:S(2)}) copy-start(bf16[1,1100,256]{2,1,0:T(8,128)(2,1)} %param.18) | copy-start | bytes 1689604
  7.2 3.4 copy-start.1
  7.2 3.4 copy-start.9
  7.2 71.3 %all-reduce.3.cloned.1.call-start = ((), (), s32[]{:S(2)}) async-start(), calls=%async_computation.3 | async-start | bytes 2097152 | tf_op jit(solution)/shard_map/psum | solution.py:44
  11.0 1.0 copy-start.6
  12.0 4.6 %copy-start.12 = (bf16[1024,2048]{1,0:T(8,128)(2,1)S(1)}, bf16[1024,2048]{1,0:T(8,128)(2,1)}, u32[]{:S(2)}) copy-start(bf16[1024,2048]{1,0:T(8,128)(2,1)} %param.15) | copy-start | bytes 12582916
  15.6 1.0 copy-start.4
  16.6 2.4 copy-start.11
  16.6 2.4 copy-start.10
  16.6 2.5 copy-start.13
  19.0 119.0 %reduce-scatter.4.cloned.1.call-start = ((), (), s32[]{:S(2)}) async-start(), calls=%async_computation.4 | async-start | bytes 40960 | tf_op jit(solution)/shard_map/reduce_scatter | solution.py:82
  19.2 61.6 %copy-start.8 = (f32[2048]{0:T(1024)S(1)}, f32[2048]{0:T(1024)}, u32[]{:S(2)}) copy-start(f32[2048]{0:T(1024)} %param.16) | copy-start | bytes 24580
  78.5 1.7 copy-start.2
  80.2 1.7 copy-start.7
  119.5 85.1 %all-reduce.5.cloned.1.call-start = ((), (), s32[]{:S(2)}) async-start(), calls=%async_computation.7 | async-start | bytes 262144 | tf_op jit(solution)/shard_map/psum | solution.py:89
  172.5 110.7 %reduce-scatter.6.cloned.1.call-start = ((), (), s32[]{:S(2)}) async-start(), calls=%async_computation.5 | async-start | bytes 5242880 | tf_op jit(solution)/shard_map/reduce_scatter | solution.py:114
  182.6 1.2 copy-start.3
  182.6 1.5 copy-start.5
  182.6 180.1 %reduce-scatter.8.cloned.1.call-start = ((), (), s32[]{:S(2)}) async-start(), calls=%async_computation.6 | async-start | bytes 5242880 | tf_op jit(solution)/shard_map/reduce_scatter | solution.py:104
Sparse Core Ops, SparseCore 0:
  19.1 59.4 all-reduce.2
  119.6 18.3 reduce-scatter.3
  172.6 31.8 all-reduce.4
  206.7 76.4 reduce-scatter.5
  285.3 77.2 reduce-scatter.7
where the time goes:
time: 372 us
  waiting for transfers between devices  242 us (65%)
  blocking collectives  67.5 us (18%)
  matrix products  20.9 us (6%)
  other arithmetic  17.3 us (5%)
  between operations  14 us (4%)
  local copies, waits for them, and re-layouts  9.53 us (3%)
    reduce_scatter x1, waiting for transfers between devices, body(): lax.psum_scatter(up_terms.astype(jnp.bfloat16), 'text', scatter_dimension...  77 us
    reduce_scatter x1, waiting for transfers between devices, body(): lax.psum_scatter(down_terms.astype(jnp.bfloat16), 'text', scatter_dimensi...  76.7 us
    psum x1, waiting for transfers between devices, body(): lax.psum(partial_out.astype(jnp.bfloat16), 'det').astype(jnp.float32)  59.4 us
    psum x1, blocking collectives, body(): feat_grad = lax.psum(feat_owned, 'det')  22.9 us
    psum x1, blocking collectives, body(): concept_feat = lax.psum(feat_part, 'det').astype(jnp.bfloat16)  22.3 us
    reduce_scatter x1, waiting for transfers between devices, body(): lax.psum_scatter(feat_terms.astype(jnp.bfloat16), 'text', scatter_dimensi...  18.4 us
    all_gather x1, blocking collectives, body(): all_feat = lax.all_gather(concept_feat, 'text', axis=0, tiled=True)  13.1 us
    psum x1, waiting for transfers between devices, body(): lax.psum(proj_part.astype(jnp.bfloat16), 'text').astype(jnp.float32)  10.8 us
  transfers between devices with their start and end apart: 5, of which 5 were waited for; matrix products, arithmetic and copies ran while one was open for 6% of the time, Pallas kernels for 0%

commit v1 on v0

--- a/solution.py
+++ b/solution.py
@@ -1,15 +1,38 @@
 import jax
 import jax.numpy as jnp
 from jax import lax
+from jax.experimental import pallas as pl
+from jax.experimental.pallas import tpu as pltpu
 from jax.sharding import PartitionSpec as P
+
 
 EPS = 1e-05
 ALPHA = 0.25
 LOGIT_BIAS = -2.0
+PACK = 128
+ROOM = 24 << 20
+LOW = jnp.bfloat16
+FULL = jnp.float32
+
+
+GELU_A = 0.7978845608028654
+GELU_B = 0.044715 * GELU_A
 
 
 def gelu_fn(values):
     return jax.nn.gelu(values, approximate=True)
+
+
+def gelu_half(values):
+    square = values * values
+    return square, 0.5 + 0.5 * jnp.tanh(values * (GELU_A + GELU_B * square))
+
+
+def gelu_both(values):
+    square, half = gelu_half(values)
+    act = values * half
+    slope = half + 2.0 * act * (1.0 - half) * (GELU_A + 3.0 * GELU_B * square)
+    return act, slope
 
 
 def focal_total(scores, target, weight):
@@ -21,7 +44,516 @@
     return jnp.sum(weight * (pos_term + neg_term))
 
 
-def body(
+def swap(values, axis, mask):
+    size = lax.axis_size(axis)
+    return lax.ppermute(values, axis, [(i, i ^ mask) for i in range(size)])
+
+
+def bit_groups(size):
+    bits = size.bit_length() - 1
+    assert size == 1 << bits
+    groups = [[0, 1]] if bits else []
+    bit = 1
+    while bit < bits:
+        wide = min(2, bits - bit)
+        groups.append([k << bit for k in range(1 << wide)])
+        bit += wide
+    return groups
+
+
+def gather_pieces(values):
+    pieces, offsets = [values], [0]
+    groups = bit_groups(lax.axis_size("det"))
+    for masks in groups[1:] + groups[:1]:
+        pieces = pieces + [swap(p, "det", m) for m in masks[1:] for p in pieces]
+        offsets = [m ^ o for m in masks for o in offsets]
+    return pieces, offsets
+
+
+def sum_det(values):
+    for masks in bit_groups(lax.axis_size("det")):
+        parts = [values] + [swap(values, "det", m) for m in masks[1:]]
+        values = sum(p.astype(FULL) for p in parts).astype(LOW)
+    return parts
+
+
+def dot_t(left, right):
+    return lax.dot_general(left, right, (((1,), (1,)), ((), ())), preferred_element_type=FULL)
+
+
+def dot_c(left, right):
+    return lax.dot_general(left, right, (((0,), (0,)), ((), ())), preferred_element_type=FULL)
+
+
+def dot_n(left, right):
+    return jnp.dot(left, right, preferred_element_type=FULL)
+
+
+def whole(array):
+    return pl.BlockSpec(array.shape, lambda *_: (0,) * len(array.shape))
+
+
+def call(kernel, grid, scalars, operands, in_specs, out_shapes, out_specs, scratch, flops):
+    moved = sum(a.size * a.dtype.itemsize for a in operands)
+    moved += sum(o.size * o.dtype.itemsize for o in out_shapes)
+    return pl.pallas_call(
+        kernel,
+        out_shape=out_shapes,
+        grid_spec=pltpu.PrefetchScalarGridSpec(
+            num_scalar_prefetch=1,
+            grid=grid,
+            in_specs=in_specs,
+            out_specs=out_specs,
+            scratch_shapes=scratch,
+        ),
+        compiler_params=pltpu.CompilerParams(dimension_semantics=("arbitrary",) * len(grid)),
+        cost_estimate=pl.CostEstimate(flops=flops, bytes_accessed=moved, transcendentals=0),
+    )(scalars, *operands)
+
+
+def shape(dims, dtype=LOW):
+    return jax.ShapeDtypeStruct(dims, dtype)
+
+
+def scatter_parts(parts, index):
+    for masks in bit_groups(lax.axis_size("det"))[1:]:
+        wide = len(masks)
+        here = lax.rem(index, wide)
+        index = lax.div(index, wide)
+        split = [p.reshape((p.shape[0] // wide, wide) + p.shape[1:]) for p in parts]
+        parts = [lax.dynamic_index_in_dim(p, here, 1, keepdims=False) for p in split]
+        for n, m in enumerate(masks[1:], 1):
+            away = sum(
+                lax.dynamic_index_in_dim(p, here ^ n, 1, keepdims=False).astype(FULL)
+                for p in split
+            )
+            parts.append(swap(away.astype(LOW), "det", m))
+    return [p[0] for p in parts]
+
+
+def front(tokens, norm_gain, w_up, w_down, scalars, cols, share, others):
+    rows, width = tokens.shape
+    units = w_up.shape[1]
+    step = min(256, units)
+    pairs = rows // share // 2
+
+    def kernel(scal, tok, gain, up, down, near_cols, far_cols, pre_t, keep, send, normed, acc):
+        n = pl.program_id(0)
+
+        @pl.when(n == 0)
+        def _():
+            x = tok[...].astype(FULL)
+            centred = x - jnp.mean(x, axis=1, keepdims=True)
+            var = jnp.mean(centred * centred, axis=1, keepdims=True)
+            normed[...] = (centred * lax.rsqrt(var + EPS) * gain[...]).astype(LOW)
+            near_cols[...] = normed[:, pl.ds(pl.multiple_of(scal[1] * cols, 128), cols)]
+            mine = pl.ds(pl.multiple_of(scal[0] * share, share), share)
+            for a in others:
+                at = pl.multiple_of((scal[1] ^ a) * cols, 128)
+                far_cols[a - 1] = normed[mine, pl.ds(at, cols)]
+
+        pre = dot_n(normed[...], up[...])
+        pre_t[...] = pre.T.astype(LOW)
+        _, half = gelu_half(pre)
+        part = dot_n((pre * half).astype(LOW), down[...])
+
+        @pl.when(n == 0)
+        def _():
+            acc[...] = part
+
+        @pl.when(n > 0)
+        def _():
+            acc[...] += part
+
+        @pl.when(n == pl.num_programs(0) - 1)
+        def _():
+            core = lax.rem(scal[0], 2)
+            for q in range(pairs):
+                at = pl.multiple_of((2 * q + core) * share, share)
+                keep[q] = acc[pl.ds(at, share), :].astype(LOW)
+                at = pl.multiple_of((2 * q + 1 - core) * share, share)
+                send[q] = acc[pl.ds(at, share), :].astype(LOW)
+
+    gain = norm_gain[None, :]
+    outs = [
+        shape((rows, cols)),
+        shape((len(others), share, cols)),
+        shape((units, rows)),
+        shape((pairs, share, width)),
+        shape((pairs, share, width)),
+    ]
+    return call(
+        kernel,
+        (units // step,),
+        scalars,
+        (tokens, gain, w_up, w_down),
+        [
+            whole(tokens),
+            whole(gain),
+            pl.BlockSpec((width, step), lambda n, _: (0, n)),
+            pl.BlockSpec((step, width), lambda n, _: (n, 0)),
+        ],
+        outs,
+        [
+            whole(outs[0]),
+            whole(outs[1]),
+            pl.BlockSpec((step, rows), lambda n, _: (n, 0)),
+            whole(outs[3]),
+            whole(outs[4]),
+        ],
+        [pltpu.VMEM((rows, width), LOW), pltpu.VMEM((rows, width), FULL)],
+        4 * rows * width * units,
+    )
+
+
+def out_norm(tokens, parts, far_cols, scalars, prompt, concepts):
+    share, width = parts[0].shape
+    cols = far_cols.shape[2]
+    count = len(parts)
+
+    def kernel(scal, tok, *refs):
+        summed = refs[0][...].astype(FULL)
+        for ref in refs[1:count]:
+            summed = summed + ref[...].astype(FULL)
+        far, near = refs[count : count + 2]
+        away = refs[count + 2 :]
+        x = tok[...].astype(FULL) + summed
+        centred = x - jnp.mean(x, axis=1, keepdims=True)
+        var = jnp.mean(centred * centred, axis=1, keepdims=True)
+        inv = lax.rsqrt(var + EPS)
+        hat = (centred * inv).astype(LOW)
+        row = lax.broadcasted_iota(jnp.int32, (share, PACK), 0) + scal[0] * share
+        lane = lax.broadcasted_iota(jnp.int32, (share, PACK), 1)
+        place = lax.rem(row, prompt)
+        concept = lax.div(row, prompt)
+        length = jnp.zeros((share, PACK), jnp.int32)
+        for c in range(concepts):
+            length = jnp.where(concept == c, scal[2 + c], length)
+        high = inv.astype(LOW).astype(FULL)
+        extras = jnp.where(lane == 0, high, 0.0)
+        extras = jnp.where(lane == 1, inv - high, extras)
+        extras = jnp.where((lane == 2) & (place < length), 1.0, extras)
+        extras = jnp.where(lane == 3, length.astype(FULL), extras).astype(LOW)
+        near[0, :, :width] = hat
+        near[0, :, width:] = extras
+        for a, ref in enumerate(away):
+            ref[:, :width] = hat
+            ref[:, width : width + PACK] = extras
+            ref[:, width + PACK :] = far[a]
+
+    outs = [
+        shape((1, share, width + PACK)),
+    ] + [shape((share, width + PACK + cols))] * far_cols.shape[0]
+    operands = (tokens, *parts, far_cols)
+    return call(
+        kernel,
+        (1,),
+        scalars,
+        operands,
+        [pl.BlockSpec((share, width), lambda n, scal: (scal[0], 0))]
+        + [whole(o) for o in operands[1:]],
+        outs,
+        [whole(o) for o in outs],
+        [],
+        20 * share * width,
+    )
+
+
+def fill(scal, pieces, offsets, held, share, start, width):
+    sources = pieces[0].shape[0]
+    rows = len(pieces) * share
+    for piece, offset in zip(pieces, offsets):
+        place = (scal[0] ^ offset) * share
+        for a in range(sources):
+            at = pl.multiple_of(start + a * rows + place, share)
+            held[pl.ds(at, share), :] = piece[a, :, :width]
+
+
+def proj_side(proj_pieces, offsets, w_down, final_gain, scalars):
+    part, query_width = proj_pieces[0].shape
+    count = len(proj_pieces)
+    width = part * count
+    units = w_down.shape[0]
+    step = min(256, units)
+
+    def kernel(scal, *refs):
+        gain, down, proj, centred, hid_t = refs[count:]
+
+        @pl.when(pl.program_id(0) == 0)
+        def _():
+            for piece, offset in zip(refs[:count], offsets):
+                at = pl.multiple_of((scal[0] ^ offset) * part, part)
+                proj[pl.ds(at, part), :] = piece[...]
+            tall = jnp.broadcast_to(gain[...], (128, width)).T
+            tall = jnp.concatenate([tall] * (query_width // 128), axis=1)
+            scaled = proj[...].astype(FULL) * tall
+            centred[...] = (scaled - jnp.mean(scaled, axis=0, keepdims=True)).astype(LOW)
+
+        hid_t[...] = dot_n(down[...], centred[...]).astype(LOW)
+
+    gain = final_gain[None, :]
+    outs = [shape((width, query_width)), shape((width, query_width)), shape((units, query_width))]
+    return call(
+        kernel,
+        (units // step,),
+        scalars,
+        (*proj_pieces, gain, w_down),
+        [whole(p) for p in proj_pieces]
+        + [whole(gain), pl.BlockSpec((step, width), lambda n, _: (n, 0))],
+        outs,
+        [whole(outs[0]), whole(outs[1]), pl.BlockSpec((step, query_width), lambda n, _: (n, 0))],
+        [],
+        2 * units * width * query_width,
+    )
+
+
+def concept_side(pieces, offsets, proj, lengths, final_gain, scalars, prompt, part):
+    _, share, packed = pieces[0].shape
+    rows = share * len(pieces)
+    width, query_width = proj.shape
+    concepts = lengths.shape[0]
+    count = len(pieces)
+
+    def kernel(scal, *refs):
+        full_proj, lens, gain, hat, feat, pooled = refs[count:]
+        fill(scal, refs[:count], offsets, hat, share, 0, packed)
+        row = lax.broadcasted_iota(jnp.int32, (concepts, rows), 1)
+        low = lax.broadcasted_iota(jnp.int32, (concepts, rows), 0) * prompt
+        pick = (row >= low) & (row < low + lens[...])
+        pick = jnp.where(pick, 1.0, 0.0).astype(LOW)
+        mean = dot_n(pick, hat[:, :width]) * gain[...] / lens[...].astype(FULL)
+        pooled[...] = mean.astype(LOW)
+        feat[:, :query_width] = dot_n(pooled[...], full_proj[...]).astype(LOW)
+        feat[:, query_width:] = pooled[:, pl.ds(pl.multiple_of(scal[0] * part, 128), part)]
+
+    gain = final_gain[None, :]
+    outs = [shape((rows, packed)), shape((concepts, query_width + part))]
+    operands = (*pieces, proj, lengths, gain)
+    return call(
+        kernel,
+        (1,),
+        scalars,
+        operands,
+        [whole(o) for o in operands],
+        outs,
+        [whole(o) for o in outs],
+        [pltpu.VMEM((concepts, width), LOW)],
+        2 * concepts * width * (rows + query_width),
+    )
+
+
+def score_side(queries, assign, allowed, feats, scalars, query_width, images):
+    count, width = queries.shape
+    groups = len(feats)
+    per_group = feats[0].shape[0]
+    concepts = groups * per_group
+    half = width // 2
+
+    def kernel(scal, query, chosen, allow, *refs):
+        grad_q, own, pooled = refs[groups : groups + 3]
+        away = refs[groups + 3 :]
+        pooled[...] = jnp.concatenate([r[:, query_width:] for r in refs[:groups]], axis=0)
+        feat = jnp.concatenate([r[:, :query_width] for r in refs[:groups]], axis=0)
+        scores = dot_t(feat, query[...]) * query_width ** (-0.5) + LOGIT_BIAS
+        slot = lax.broadcasted_iota(jnp.int32, (concepts, 1), 0)
+        ident = (scal[1] ^ lax.div(slot, per_group)) * per_group + lax.rem(slot, per_group)
+        small = jnp.exp(-jnp.abs(scores))
+        logs = jnp.log1p(small)
+        over = 1.0 / (1.0 + small)
+        under = small * over
+        up = scores >= 0
+        prob = jnp.where(up, over, under)
+        rest = jnp.where(up, under, over)
+        log_pos = jnp.minimum(scores, 0.0) - logs
+        log_neg = jnp.minimum(-scores, 0.0) - logs
+        pos = ALPHA * rest * rest * (2.0 * prob * log_pos - rest)
+        neg = (1.0 - ALPHA) * prob * prob * (prob - 2.0 * rest * log_neg)
+        grad = jnp.where(chosen[...] == ident, pos, neg) * allow[...]
+        grad = grad.astype(LOW)
+        terms = dot_n(grad, query[...]) * (query_width ** (-0.5) / images)
+        terms = terms.astype(LOW)
+        own[...] = terms
+        for a in range(1, groups):
+            for b in range(groups):
+                block = (a ^ b) * per_group
+                away[a - 1][b * per_group : (b + 1) * per_group, :] = terms[
+                    block : block + per_group
+                ]
+        back = dot_c(grad, feat) * query_width ** (-0.5)
+        grad_q[pl.ds(0, count, 2), :] = back[:, :half]
+        grad_q[pl.ds(1, count, 2), :] = back[:, half:]
+
+    outs = [
+        shape((2 * count, half), FULL),
+        shape((concepts, width)),
+        shape((concepts, feats[0].shape[1] - query_width)),
+    ] + [shape((concepts, width))] * (groups - 1)
+    operands = (queries, assign, allowed, *feats)
+    return call(
+        kernel,
+        (1,),
+        scalars,
+        operands,
+        [whole(o) for o in operands],
+        outs,
+        [whole(o) for o in outs],
+        [],
+        6 * count * width * concepts,
+    )
+
+
+def back_side(hat_near, cols_near, pieces, offsets, w_down, centred, scalars, cols):
+    sources, share, _ = pieces[0].shape
+    near_rows, hat_width = hat_near.shape
+    rows = near_rows + sources * share * len(pieces)
+    units, width = w_down.shape
+    query_width = centred.shape[1]
+    step = min(256, units)
+    count = len(pieces)
+
+    def kernel(scal, near, near_cols, *refs):
+        down, proj = refs[count : count + 2]
+        back_t, along, part, facts, normed_t, held, held_cols = refs[count + 2 :]
+
+        @pl.when(pl.program_id(0) == 0)
+        def _():
+            held[:near_rows, :] = near[...]
+            held_cols[:near_rows, :] = near_cols[...]
+            for piece, offset in zip(refs[:count], offsets):
+                place = (scal[0] ^ offset) * share
+                for a in range(sources):
+                    at = pl.multiple_of(near_rows + a * share * count + place, share)
+                    held[pl.ds(at, share), :] = piece[a, :, :hat_width]
+                    held_cols[pl.ds(at, share), :] = piece[a, :, hat_width:]
+            part[...] = held[:, pl.ds(pl.multiple_of(scal[1] * cols, 128), cols)]
+            facts[...] = held[:, width:]
+            along[...] = dot_n(held[:, :width], proj[...]).astype(LOW)
+            normed_t[...] = held_cols[...].T
+
+        back_t[...] = dot_t(down[...], held[:, :width]).astype(LOW)
+
+    outs = [
+        shape((units, rows)),
+        shape((rows, query_width)),
+        shape((rows, cols)),
+        shape((rows, hat_width - width)),
+        shape((cols, rows)),
+    ]
+    operands = (hat_near, cols_near, *pieces, w_down, centred)
+    return call(
+        kernel,
+        (units // step,),
+        scalars,
+        operands,
+        [whole(o) for o in operands[:-2]]
+        + [pl.BlockSpec((step, width), lambda n, _: (n, 0)), whole(centred)],
+        outs,
+        [pl.BlockSpec((step, rows), lambda n, _: (n, 0))] + [whole(o) for o in outs[1:]],
+        [pltpu.VMEM((rows, hat_width), LOW), pltpu.VMEM((rows, cols), LOW)],
+        2 * rows * width * (units + query_width),
+    )
+
+
+def late(feats, pooled, hid_t, centred, facts, along, back_t, hat_cols, normed_t, pre, scalars, prompt):
+    rows, cols = hat_cols.shape
+    units, query_width = hid_t.shape
+    concepts = feats[0].shape[0]
+    part = pooled.shape[1]
+    wide = len(feats)
+    step = min(256, units)
+    model = centred.shape[0]
+    groups = len(pre)
+    per = rows // groups
+
+    def kernel(scal, pool, hid, cent, facts, along, back, hat, normed, *refs):
+        pre_refs, feat_refs = refs[:groups], refs[groups : groups + wide]
+        up, down, proj, feat, out_grad, grad_t, act_t, weights = refs[groups + wide :]
+        row = lax.broadcasted_iota(jnp.int32, (rows, concepts), 0)
+        low = lax.broadcasted_iota(jnp.int32, (rows, concepts), 1) * prompt
+        pick = jnp.where((row >= low) & (row < low + prompt), 1.0, 0.0).astype(LOW)
+
+        @pl.when(pl.program_id(0) == 0)
+        def _():
+            total = sum(r[...].astype(FULL) for r in feat_refs)
+            feat[...] = total.astype(LOW)
+            proj[...] = lax.dot_general(
+                pool[...].astype(FULL),
+                total,
+                (((0,), (0,)), ((), ())),
+                precision=lax.Precision.HIGHEST,
+                preferred_element_type=FULL,
+            )
+            known = facts[...].astype(FULL)
+            inv = known[:, 0:1] + known[:, 1:2]
+            lead = inv * known[:, 2:3] / known[:, 3:4]
+            chosen = dot_n(pick, feat[...])
+            second = jnp.sum(along[...].astype(FULL) * chosen, axis=1, keepdims=True)
+            tail = lead * second * (1.0 / model)
+            at = pl.multiple_of(scal[1] * cols, 128)
+            grad_cols = dot_t(feat[...], cent[pl.ds(at, cols), :]).astype(LOW)
+            out_grad[...] = (
+                lead * dot_n(pick, grad_cols) - tail * hat[...].astype(FULL)
+            ).astype(LOW)
+            lane = lax.broadcasted_iota(jnp.int32, (rows, 128), 1)
+            both = jnp.where(lane == 0, lead, jnp.where(lane == 1, tail, 0.0))
+            weights[...] = both.T[:8]
+
+        lead = weights[0:1, :]
+        tail = weights[1:2, :]
+        grad_step = dot_t(hid[...], feat[...]).astype(LOW)
+        grad_rows = lead * dot_t(grad_step, pick) - tail * back[...].astype(FULL)
+        for g in range(groups):
+            act, slope = gelu_both(pre_refs[g][...].astype(FULL))
+            span = slice(g * per, (g + 1) * per)
+            act_t[:, span] = act.astype(LOW)
+            grad_t[:, span] = (slope * grad_rows[:, span]).astype(LOW)
+        up[...] = dot_t(normed[...], grad_t[...])
+        down[...] = dot_n(act_t[...], out_grad[...])
+
+    outs = [
+        shape((cols, units), FULL),
+        shape((units, cols), FULL),
+        shape((part, query_width), FULL),
+    ]
+    operands = (
+        pooled, hid_t, centred, facts, along, back_t, hat_cols, normed_t, *pre, *feats
+    )
+    moving = lambda wide: pl.BlockSpec((step, wide), lambda n, _: (n, 0))
+    return call(
+        kernel,
+        (units // step,),
+        scalars,
+        operands,
+        [
+            whole(pooled),
+            moving(query_width),
+            whole(centred),
+            whole(facts),
+            whole(along),
+            moving(rows),
+            whole(hat_cols),
+            whole(normed_t),
+        ]
+        + [moving(per)] * groups
+        + [whole(f) for f in feats],
+        outs,
+        [
+            pl.BlockSpec((cols, step), lambda n, _: (0, n)),
+            pl.BlockSpec((step, cols), lambda n, _: (n, 0)),
+            whole(outs[2]),
+        ],
+        [
+            pltpu.VMEM((concepts, query_width), LOW),
+            pltpu.VMEM((rows, cols), LOW),
+            pltpu.VMEM((step, rows), LOW),
+            pltpu.VMEM((step, rows), LOW),
+            pltpu.VMEM((8, rows), FULL),
+        ],
+        4 * rows * units * cols,
+    )
+
+
+def body_scatter(
     prompt_embeds, prompt_len, norm_gain, w_up, w_down, final_gain, w_proj, queries, assign, valid
 ):
     per_group, prompt, model_width = prompt_embeds.shape
@@ -117,6 +649,71 @@
     return (up_grad, down_grad, proj_grad, query_grad.reshape(img_count, query_count, query_width))
 
 
+def body(
+    prompt_embeds, prompt_len, norm_gain, w_up, w_down, final_gain, w_proj, queries, assign, valid
+):
+    per_group, prompt, width = prompt_embeds.shape
+    tok_rows = per_group * prompt
+    det_size = lax.axis_size("det")
+    text_size = lax.axis_size("text")
+    det = lax.axis_index("det")
+    text = lax.axis_index("text")
+    if 4 * text_size * tok_rows * width * 2 > ROOM or queries.shape[0] > 1:
+        return body_scatter(
+            prompt_embeds, prompt_len, norm_gain, w_up, w_down, final_gain, w_proj, queries,
+            assign, valid
+        )
+    share = tok_rows // det_size
+    cols = width // text_size
+    part = width // det_size
+    others = list(range(1, text_size))
+    scalars = jnp.concatenate([jnp.stack([det, text]).astype(jnp.int32), prompt_len])
+    tokens = prompt_embeds.reshape(tok_rows, width)
+
+    cols_near, cols_far, pre_near, keep, send = front(
+        tokens, norm_gain, w_up, w_down, scalars, cols, share, others
+    )
+    parts = scatter_parts([keep, swap(send, "det", 1)], lax.div(det, 2))
+    proj_pieces, offsets = gather_pieces(w_proj)
+    proj, scaled_proj, hid_t = proj_side(proj_pieces, offsets, w_down, final_gain, scalars)
+    pre = [pre_near] + [swap(pre_near, "text", a) for a in others]
+
+    packed, *packed_far = out_norm(tokens, parts, cols_far, scalars, prompt, per_group)
+    near_pieces, _ = gather_pieces(packed)
+    far = jnp.stack([swap(packed_far[a - 1], "text", a) for a in others])
+    far_pieces, _ = gather_pieces(far)
+
+    hat_near, feats = concept_side(
+        near_pieces, offsets, proj, prompt_len[:, None], final_gain, scalars, prompt, part
+    )
+    feats = [feats] + [swap(feats, "text", a) for a in others]
+    img_count, query_count, query_width = queries.shape
+
+    blocks = valid.astype(FULL).reshape(text_size, per_group)
+    allowed = jnp.concatenate(
+        [lax.dynamic_slice_in_dim(blocks, text ^ a, 1, 0) for a in range(text_size)], 0
+    ).reshape(text_size * per_group, 1)
+    images = img_count * text_size * det_size
+    query_grad, terms, pooled, *away = score_side(
+        queries.reshape(query_count, query_width), assign, allowed, feats, scalars,
+        query_width, images
+    )
+
+    total = terms.astype(FULL)
+    for a in others:
+        total = total + swap(away[a - 1], "text", a).astype(FULL)
+    feat_parts = sum_det(total.astype(LOW))
+
+    back_t, along, hat_cols, facts, normed_t = back_side(
+        hat_near, cols_near, far_pieces, offsets, w_down, scaled_proj, scalars, cols
+    )
+    up_grad, down_grad, proj_grad = late(
+        feat_parts, pooled, hid_t, scaled_proj, facts, along, back_t, hat_cols, normed_t, pre,
+        scalars, prompt
+    )
+    return (up_grad, down_grad, proj_grad, query_grad.reshape(img_count, query_count, query_width))
+
+
 def solution(mesh):
     return jax.shard_map(
         body,

time: 372 us -> 152 us (0.41)
  waiting for transfers between devices: 242 us -> 40.5 us
  blocking collectives: 67.5 us -> 0 us
  Pallas kernels: 0 us -> 53.3 us
  starting transfers between devices: 0.39 us -> 46.1 us
  matrix products: 20.9 us -> 0 us
  other arithmetic: 17.3 us -> 3.22 us
  between operations: 14 us -> 1.14 us
    reduce_scatter x3 -> x0, waiting for transfers between devices: 172 us -> none  [the longest x1 77 us: body(): lax.psum_scatter(up_terms.astype(jnp.bfloat16), 'text', scatter_dimension...]
    psum x2 -> x0, waiting for transfers between devices: 70.2 us -> none  [the longest x1 59.4 us: body(): lax.psum(partial_out.astype(jnp.bfloat16), 'det').astype(jnp.float32)]
    pallas_call x0 -> x7, Pallas kernels: none -> 53.3 us  [call(): pl.pallas_call(kernel, out_shape=out_shapes, grid_spec=pltpu.PrefetchScal...]
    ppermute x0 -> x41, starting transfers between devices: none -> 46.1 us  [swap(): return lax.ppermute(values, axis, [(i, i ^ mask) for i in range(size)])]
    psum x2 -> x0, blocking collectives: 45.2 us -> none  [the longest x1 22.9 us: body(): feat_grad = lax.psum(feat_owned, 'det')]
    ppermute x0 -> x41, waiting for transfers between devices: none -> 40.5 us  [swap(): return lax.ppermute(values, axis, [(i, i ^ mask) for i in range(size)])]
    all_gather x2 -> x0, blocking collectives: 22.3 us -> none  [the longest x1 13.1 us: body(): all_feat = lax.all_gather(concept_feat, 'text', axis=0, tiled=True)]
    dot_general x10 -> x0, matrix products: 20.9 us -> none  [the longest x1 7.92 us: body(): lax.dot_general(normed, pre_grad, (((0,), (0,)), ((), ())), preferred_ele...]
  transfers between devices with their start and end apart: 5 -> 41, of which waited for: 5 -> 12; matrix products, arithmetic and copies ran while one was open for 6% -> 4% of each run, Pallas kernels for 0% -> 19%
where the time goes in v1:
time: 152 us; the launch traced here: 151 us
  Pallas kernels  53.3 us (35%)
  starting transfers between devices  46.1 us (30%)
  waiting for transfers between devices  40.5 us (27%)
  local copies, waits for them, and re-layouts  7.18 us (5%)
  other arithmetic  3.22 us (2%)
    pallas_call x7, Pallas kernels, call(): pl.pallas_call(kernel, out_shape=out_shapes, grid_spec=pltpu.PrefetchScal...  53.3 us
    ppermute x41, starting transfers between devices, swap(): return lax.ppermute(values, axis, [(i, i ^ mask) for i in range(size)])  46.1 us
    ppermute x41, waiting for transfers between devices, swap(): return lax.ppermute(values, axis, [(i, i ^ mask) for i in range(size)])  40.5 us
    unnamed x74, local copies, waits for them, and re-layouts  3.47 us
  transfers between devices with their start and end apart: 41, of which 12 were waited for; matrix products, arithmetic and copies ran while one was open for 4% of the time, Pallas kernels for 19%

profile of v1, /device:TPU:0, one launch (start us, length us, event | category | flops | bytes accessed | tf_op | source)
XLA Modules:
  0.0 151.5 jit_solution(12656644119914493267)
XLA Ops:
  0.6 1.2 pad_add_fusion.scal
  1.8 10.7 %shard_map.129 = (bf16[256,512]{1,0:T(8,128)(2,1)}, bf16[3,32,512]{2,1,0:T(8,128)(2,1)}, bf16[1024,256]{1,0:T(8,128)(2,1)}, bf16[4,32,2048]{2,1,0:T(8,128)(2,1)}, bf16[4,32,2048]{2,1,0:T(8,128)(2,1)}) custom-call(s32[18]{0:T(128)} %pad_add_fusion.scal, bf16[256,2048]{1,0:T(8,128)(2,1)} %bitcast.18, f32[1,2048]{1,0:T(1,128)} %bitcast.29, ...), custom_call_target="tpu_custom_call" | custom-call | flops 2147483648 | bytes 11378688 | tf_op jit(solution)/shard_map/pallas_call | solution.py:99
  12.6 0.6 collective-permute-start
  13.2 3.5 %collective-permute-start.13 = (bf16[256,256]{1,0:T(8,128)(2,1)S(1)}, bf16[256,256]{1,0:T(8,128)(2,1)S(1)}, u32[]{:S(2)}, u32[]{:S(2)}) collective-permute-start(bf16[256,256]{1,0:T(8,128)(2,1)S(1)} %copy-done.14), channel_id=1, source_target_pairs={{0,6},{1,7},{2,4},{3,5},{4,2},{5,3},{6,0},{7,1},{8,14},{9,15},{10,... | collective-permute-start | bytes 393224 | tf_op jit(solution)/shard_map/ppermute | solution.py:49
  17.3 1.1 add_convert_fusion
  18.5 2.9 %collective-permute-start.3 = (bf16[1,32,2048]{2,1,0:T(8,128)(2,1)S(1)}, bf16[1,32,2048]{2,1,0:T(8,128)(2,1)S(1)}, u32[]{:S(2)}, u32[]{:S(2)}) collective-permute-start(bf16[1,32,2048]{2,1,0:T(8,128)(2,1)S(1)} %get-tuple-element.68), channel_id=1, source_target_pairs={{0,6},{1,7},{2,4},{3,5},{4,2},{5,3},{6,0},{7,1},{8,14},{9,15},{10,... | collective-permute-start | bytes 393224 | tf_op jit(solution)/shard_map/ppermute | solution.py:49
  21.4 1.6 %dynamic-slice_bitcast_fusion.1.refs_0_ = bf16[32,2048]{1,0:T(8,128)(2,1)} fusion(bf16[4,32,2048]{2,1,0:T(8,128)(2,1)} %get-tuple-element.32, s32[]{:T(128)S(6)} %select_n.33), kind=kLoop, calls=%fused_computation.5 | loop fusion | bytes 262148 | tf_op jit(solution)/shard_map/squeeze | solution.py:131
  23.4 3.0 %collective-permute-done.3 = bf16[1,32,2048]{2,1,0:T(8,128)(2,1)S(1)} collective-permute-done((bf16[1,32,2048]{2,1,0:T(8,128)(2,1)S(1)}, bf16[1,32,2048]{2,1,0:T(8,128)(2,1)S(1)}, u32[]{:S(2)}, u32[]{:S(2)}) %collective-permute-start.3) | collective-permute-done | bytes 131104 | tf_op jit(solution)/shard_map/ppermute | solution.py:49
  26.5 1.7 %collective-permute-start.1 = (bf16[1,32,2048]{2,1,0:T(8,128)(2,1)S(1)}, bf16[1,32,2048]{2,1,0:T(8,128)(2,1)S(1)}, u32[]{:S(2)}, u32[]{:S(2)}) collective-permute-start(bf16[1,32,2048]{2,1,0:T(8,128)(2,1)S(1)} %get-tuple-element.70), channel_id=1, source_target_pairs={{0,2},{1,3},{2,0},{3,1},{4,6},{5,7},{6,4},{7,5},{8,10},{9,11},{10,... | collective-permute-start | bytes 393224 | tf_op jit(solution)/shard_map/ppermute | solution.py:49
  28.2 0.7 dynamic-slice_bitcast_fusion.refs_1_
  29.2 2.3 %collective-permute-done.1 = bf16[1,32,2048]{2,1,0:T(8,128)(2,1)S(1)} collective-permute-done((bf16[1,32,2048]{2,1,0:T(8,128)(2,1)S(1)}, bf16[1,32,2048]{2,1,0:T(8,128)(2,1)S(1)}, u32[]{:S(2)}, u32[]{:S(2)}) %collective-permute-start.1) | collective-permute-done | bytes 131104 | tf_op jit(solution)/shard_map/ppermute | solution.py:49
  31.4 0.6 copy-done.24
  32.1 3.0 %shard_map.130 = (bf16[1,32,2176]{2,1,0:T(8,128)(2,1)}, bf16[32,2688]{1,0:T(8,128)(2,1)}, bf16[32,2688]{1,0:T(8,128)(2,1)}, bf16[32,2688]{1,0:T(8,128)(2,1)}) custom-call(s32[18]{0:T(128)} %pad_add_fusion.scal, bf16[256,2048]{1,0:T(8,128)(2,1)} %bitcast.19, bf16[32,2048]{1,0:T(8,128)(2,1)} %dynamic-slice_bitcast_fusion.1.refs_0_, ...), custom_call_target="tpu_custom_call" | custom-call | flops 1310720 | bytes 2457600 | tf_op jit(solution)/shard_map/pallas_call | solution.py:99
  35.1 2.7 %collective-permute-start.6 = (bf16[1,32,2176]{2,1,0:T(8,128)(2,1)}, bf16[1,32,2176]{2,1,0:T(8,128)(2,1)S(1)}, u32[]{:S(2)}, u32[]{:S(2)}) collective-permute-start(bf16[1,32,2176]{2,1,0:T(8,128)(2,1)} %get-tuple-element.35.refs_0_), channel_id=1, source_target_pairs={{0,6},{1,7},{2,4},{3,5},{4,2},{5,3},{6,0},{7,1},{8,14},{9,15},{10,... | collective-permute-start | bytes 417800 | tf_op jit(solution)/shard_map/ppermute | solution.py:49
  40.0 1.8 %collective-permute-start.21 = (bf16[32,2688]{1,0:T(8,128)(2,1)}, bf16[32,2688]{1,0:T(8,128)(2,1)S(1)}, u32[]{:S(2)}, u32[]{:S(2)}) collective-permute-start(bf16[32,2688]{1,0:T(8,128)(2,1)} %get-tuple-element.43), channel_id=1, source_target_pairs={{0,8},{8,0},{16,24},{24,16},{1,9},{9,1},{17,25},{25,17},{2,10},{10... | collective-permute-start | bytes 516104 | tf_op jit(solution)/shard_map/ppermute | solution.py:49
  41.8 2.6 %collective-permute-start.22 = (bf16[32,2688]{1,0:T(8,128)(2,1)}, bf16[32,2688]{1,0:T(8,128)(2,1)S(1)}, u32[]{:S(2)}, u32[]{:S(2)}) collective-permute-start(bf16[32,2688]{1,0:T(8,128)(2,1)} %get-tuple-element.44), channel_id=1, source_target_pairs={{0,16},{8,24},{16,0},{24,8},{1,17},{9,25},{17,1},{25,9},{2,18},{10... | collective-permute-start | bytes 516104 | tf_op jit(solution)/shard_map/ppermute | solution.py:49
  44.4 0.7 collective-permute-start.23
  45.2 0.7 copy.17.refs_9_
  46.0 7.0 %shard_map.131 = (bf16[2048,256]{1,0:T(8,128)(2,1)}, bf16[2048,256]{1,0:T(8,128)(2,1)}, bf16[1024,256]{1,0:T(8,128)(2,1)}) custom-call(s32[18]{0:T(128)} %pad_add_fusion.scal, bf16[256,256]{1,0:T(8,128)(2,1)} %refs_0_.1, bf16[256,256]{1,0:T(8,128)(2,1)} %copy-done.17, bf16[256,256]{1,0:T(8,128)(2,1)} %copy-done.16, bf16[256,256]{1,0:T(8,128)(2,1)} %copy-done.15, ...), custom_call_target="tpu_custom_call" | custom-call | flops 1073741824 | bytes 7872512 | tf_op jit(solution)/shard_map/pallas_call | solution.py:99
  53.0 0.5 collective-permute-start.10
  53.7 3.8 %collective-permute-done.22 = bf16[32,2688]{1,0:T(8,128)(2,1)S(1)} collective-permute-done((bf16[32,2688]{1,0:T(8,128)(2,1)}, bf16[32,2688]{1,0:T(8,128)(2,1)S(1)}, u32[]{:S(2)}, u32[]{:S(2)}) %collective-permute-start.22) | collective-permute-done | bytes 172064 | tf_op jit(solution)/shard_map/ppermute | solution.py:49
  57.6 2.6 %collective-permute-start.26 = (bf16[3,32,2688]{2,1,0:T(8,128)(2,1)S(1)}, bf16[3,32,2688]{2,1,0:T(8,128)(2,1)S(1)}, u32[]{:S(2)}, u32[]{:S(2)}) collective-permute-start(bf16[3,32,2688]{2,1,0:T(8,128)(2,1)S(1)} %pad_maximum_fusion.refs_0_), channel_id=1, source_target_pairs={{0,6},{1,7},{2,4},{3,5},{4,2},{5,3},{6,0},{7,1},{8,14},{9,15},{10,... | collective-permute-start | bytes 1548296 | tf_op jit(solution)/shard_map/ppermute | solution.py:49
  61.9 3.5 %shard_map.132 = (bf16[256,2176]{1,0:T(8,128)(2,1)}, bf16[16,512]{1,0:T(8,128)(2,1)}) custom-call(s32[18]{0:T(128)} %pad_add_fusion.scal, bf16[1,32,2176]{2,1,0:T(8,128)(2,1)} %get-tuple-element.35.refs_0_, bf16[1,32,2176]{2,1,0:T(8,128)(2,1)} %copy-done.8, bf16[1,32,2176]{2,1,0:T(8,128)(2,1)} %copy-done.7, bf16[1,32,2176]{2,1,0:T(8,128)(2,1)} %copy-done.6, ...), custom_call_target="tpu_custom_call" | custom-call | flops 33554432 | bytes 3301440 | tf_op jit(solution)/shard_map/pallas_call | solution.py:99
  65.4 2.3 %collective-permute-start.20 = (bf16[16,512]{1,0:T(8,128)(2,1)}, bf16[16,512]{1,0:T(8,128)(2,1)S(1)}, u32[]{:S(2)}, u32[]{:S(2)}) collective-permute-start(bf16[16,512]{1,0:T(8,128)(2,1)} %get-tuple-element.37.refs_0_), channel_id=1, source_target_pairs={{0,24},{8,16},{16,8},{24,0},{1,25},{9,17},{17,9},{25,1},{2,26},{10... | collective-permute-start | bytes 49160 | tf_op jit(solution)/shard_map/ppermute | solution.py:49
  67.8 2.0 %collective-permute-start.19 = (bf16[16,512]{1,0:T(8,128)(2,1)}, bf16[16,512]{1,0:T(8,128)(2,1)S(1)}, u32[]{:S(2)}, u32[]{:S(2)}) collective-permute-start(bf16[16,512]{1,0:T(8,128)(2,1)} %get-tuple-element.37.refs_0_), channel_id=1, source_target_pairs={{0,16},{8,24},{16,0},{24,8},{1,17},{9,25},{17,1},{25,9},{2,18},{10... | collective-permute-start | bytes 49160 | tf_op jit(solution)/shard_map/ppermute | solution.py:49
  69.8 1.5 collective-permute-done.20.refs_3_
  71.3 0.9 collective-permute-start.18
  72.2 0.7 reshape.66.allow
  72.9 2.3 %collective-permute-done.18.refs_1_ = bf16[16,512]{1,0:T(8,128)(2,1)S(1)} collective-permute-done((bf16[16,512]{1,0:T(8,128)(2,1)}, bf16[16,512]{1,0:T(8,128)(2,1)S(1)}, u32[]{:S(2)}, u32[]{:S(2)}) %collective-permute-start.18) | collective-permute-done | bytes 16416 | tf_op jit(solution)/shard_map/ppermute | solution.py:49
  75.2 0.6 copy-done.30
  75.8 3.6 %shard_map.133 = (f32[2200,128]{1,0:T(8,128)}, bf16[64,256]{1,0:T(8,128)(2,1)}, bf16[64,256]{1,0:T(8,128)(2,1)}, bf16[64,256]{1,0:T(8,128)(2,1)}, bf16[64,256]{1,0:T(8,128)(2,1)}, /*index=5*/bf16[64,256]{1,0:T(8,128)(2,1)}) custom-call(s32[18]{0:T(128)} %pad_add_fusion.scal, bf16[1100,256]{1,0:T(8,128)(2,1)} %bitcast.20, s32[1,1100]{1,0:T(1,128)} %chosen.1, ...), custom_call_target="tpu_custom_call" | custom-call | flops 108134400 | bytes 1923632 | tf_op jit(solution)/shard_map/pallas_call | solution.py:99
  79.5 0.9 collective-permute-start.34
  80.4 1.9 %collective-permute-start.35 = (bf16[64,256]{1,0:T(8,128)(2,1)}, bf16[64,256]{1,0:T(8,128)(2,1)S(1)}, u32[]{:S(2)}, u32[]{:S(2)}) collective-permute-start(bf16[64,256]{1,0:T(8,128)(2,1)} %get-tuple-element.54), channel_id=1, source_target_pairs={{0,16},{8,24},{16,0},{24,8},{1,17},{9,25},{17,1},{25,9},{2,18},{10... | collective-permute-start | bytes 98312 | tf_op jit(solution)/shard_map/ppermute | solution.py:49
  82.2 1.3 collective-permute-done.34
  83.6 2.2 %collective-permute-start.33 = (bf16[1024,256]{1,0:T(8,128)(2,1)S(1)}, bf16[1024,256]{1,0:T(8,128)(2,1)S(1)}, u32[]{:S(2)}, u32[]{:S(2)}) collective-permute-start(bf16[1024,256]{1,0:T(8,128)(2,1)S(1)} %copy-done), channel_id=1, source_target_pairs={{0,24},{8,16},{16,8},{24,0},{1,25},{9,17},{17,9},{25,1},{2,26},{10... | collective-permute-start | bytes 1572872 | tf_op jit(solution)/shard_map/ppermute | solution.py:49
  85.8 11.9 %collective-permute-done.35 = bf16[64,256]{1,0:T(8,128)(2,1)S(1)} collective-permute-done((bf16[64,256]{1,0:T(8,128)(2,1)}, bf16[64,256]{1,0:T(8,128)(2,1)S(1)}, u32[]{:S(2)}, u32[]{:S(2)}) %collective-permute-start.35) | collective-permute-done | bytes 32800 | tf_op jit(solution)/shard_map/ppermute | solution.py:49
  97.7 2.3 %collective-permute-start.36 = (bf16[64,256]{1,0:T(8,128)(2,1)}, bf16[64,256]{1,0:T(8,128)(2,1)S(1)}, u32[]{:S(2)}, u32[]{:S(2)}) collective-permute-start(bf16[64,256]{1,0:T(8,128)(2,1)} %get-tuple-element.55), channel_id=1, source_target_pairs={{0,24},{8,16},{16,8},{24,0},{1,25},{9,17},{17,9},{25,1},{2,26},{10... | collective-permute-start | bytes 98312 | tf_op jit(solution)/shard_map/ppermute | solution.py:49
  99.9 3.7 %collective-permute-done.36 = bf16[64,256]{1,0:T(8,128)(2,1)S(1)} collective-permute-done((bf16[64,256]{1,0:T(8,128)(2,1)}, bf16[64,256]{1,0:T(8,128)(2,1)S(1)}, u32[]{:S(2)}, u32[]{:S(2)}) %collective-permute-start.36) | collective-permute-done | bytes 32800 | tf_op jit(solution)/shard_map/ppermute | solution.py:49
  104.7 0.8 add_convert_fusion.4
  105.7 2.2 %collective-permute-done.37 = bf16[64,256]{1,0:T(8,128)(2,1)S(1)} collective-permute-done((bf16[64,256]{1,0:T(8,128)(2,1)S(1)}, bf16[64,256]{1,0:T(8,128)(2,1)S(1)}, u32[]{:S(2)}, u32[]{:S(2)}) %collective-permute-start.37) | collective-permute-done | bytes 32800 | tf_op jit(solution)/shard_map/ppermute | solution.py:49
  107.8 5.1 %collective-permute-start.32 = (bf16[1024,256]{1,0:T(8,128)(2,1)S(1)}, bf16[1024,256]{1,0:T(8,128)(2,1)S(1)}, u32[]{:S(2)}, u32[]{:S(2)}) collective-permute-start(bf16[1024,256]{1,0:T(8,128)(2,1)S(1)} %copy-done), channel_id=1, source_target_pairs={{0,16},{8,24},{16,0},{24,8},{1,17},{9,25},{17,1},{25,9},{2,18},{10... | collective-permute-start | bytes 1572872 | tf_op jit(solution)/shard_map/ppermute | solution.py:49
  113.0 2.4 %collective-permute-start.40 = (bf16[64,256]{1,0:T(8,128)(2,1)S(1)}, bf16[64,256]{1,0:T(8,128)(2,1)S(1)}, u32[]{:S(2)}, u32[]{:S(2)}) collective-permute-start(bf16[64,256]{1,0:T(8,128)(2,1)S(1)} %add_convert_fusion.3.refs_4_), channel_id=1, source_target_pairs={{0,6},{1,7},{2,4},{3,5},{4,2},{5,3},{6,0},{7,1},{8,14},{9,15},{10,... | collective-permute-start | bytes 98312 | tf_op jit(solution)/shard_map/ppermute | solution.py:49
  115.4 0.6 collective-permute-start.39
  116.2 0.5 collective-permute-start.38
  117.0 11.7 %shard_map.134 = (bf16[1024,1024]{1,0:T(8,128)(2,1)}, bf16[1024,256]{1,0:T(8,128)(2,1)}, bf16[1024,512]{1,0:T(8,128)(2,1)}, bf16[1024,128]{1,0:T(8,128)(2,1)}, bf16[512,1024]{1,0:T(8,128)(2,1)}) custom-call(s32[18]{0:T(128)} %pad_add_fusion.scal, bf16[256,2176]{1,0:T(8,128)(2,1)} %get-tuple-element.41.near, bf16[256,512]{1,0:T(8,128)(2,1)} %get-tuple-element.42.near_cols, ...), custom_call_target="tpu_custom_call" | custom-call | flops 5368709120 | bytes 15728640 | tf_op jit(solution)/shard_map/pallas_call | solution.py:99
  128.7 7.7 %collective-permute-done.32.refs_2_ = bf16[1024,256]{1,0:T(8,128)(2,1)S(1)} collective-permute-done((bf16[1024,256]{1,0:T(8,128)(2,1)S(1)}, bf16[1024,256]{1,0:T(8,128)(2,1)S(1)}, u32[]{:S(2)}, u32[]{:S(2)}) %collective-permute-start.32) | collective-permute-done | bytes 524320 | tf_op jit(solution)/shard_map/ppermute | solution.py:49
  136.5 0.8 copy-done.2
  137.6 13.8 %shard_map.135 = (f32[512,1024]{1,0:T(8,128)}, f32[1024,512]{1,0:T(8,128)}, f32[256,256]{1,0:T(8,128)}) custom-call(s32[18]{0:T(128)} %pad_add_fusion.scal, bf16[64,256]{1,0:T(8,128)(2,1)} %get-tuple-element.38.pool, bf16[1024,256]{1,0:T(8,128)(2,1)} %get-tuple-element.39.hid, bf16[2048,256]{1,0:T(8,128)(2,1)} %get-tuple-element.40.refs_9_.cent, ...), custom_call_target="tpu_custom_call" | custom-call | flops 2147483648 | bytes 13271040 | tf_op jit(solution)/shard_map/pallas_call | solution.py:99
  (128 shorter events, 7.7 us)
Async XLA Ops:
  12.6 32.5 %copy-start.36 = (s32[1,64]{1,0:T(1,128)S(1)}, s32[1,64]{1,0:T(1,128)}, u32[]{:S(2)}) copy-start(s32[1,64]{1,0:T(1,128)} %param.19) | copy-start | bytes 772
  12.6 32.6 %copy-start.31 = (s32[16]{0:T(128)S(1)}, s32[16]{0:T(128)}, u32[]{:S(2)}) copy-start(s32[16]{0:T(128)} %param.11) | copy-start | bytes 196
  12.6 4.7 %collective-permute-start = (bf16[4,32,2048]{2,1,0:T(8,128)(2,1)}, bf16[4,32,2048]{2,1,0:T(8,128)(2,1)S(1)}, u32[]{:S(2)}, u32[]{:S(2)}) collective-permute-start(bf16[4,32,2048]{2,1,0:T(8,128)(2,1)} %get-tuple-element.33), channel_id=1, source_target_pairs={{0,1},{1,0},{2,3},{3,2},{4,5},{5,4},{6,7},{7,6},{8,9},{9,8},{10,11... | collective-permute-start | bytes 1572872 | tf_op jit(solution)/shard_map/ppermute | solution.py:49
  13.2 24.7 %collective-permute-start.13 = (bf16[256,256]{1,0:T(8,128)(2,1)S(1)}, bf16[256,256]{1,0:T(8,128)(2,1)S(1)}, u32[]{:S(2)}, u32[]{:S(2)}) collective-permute-start(bf16[256,256]{1,0:T(8,128)(2,1)S(1)} %copy-done.14), channel_id=1, source_target_pairs={{0,6},{1,7},{2,4},{3,5},{4,2},{5,3},{6,0},{7,1},{8,14},{9,15},{10,... | collective-permute-start | bytes 393224 | tf_op jit(solution)/shard_map/ppermute | solution.py:49
  16.7 21.7 %collective-permute-start.12 = (bf16[256,256]{1,0:T(8,128)(2,1)S(1)}, bf16[256,256]{1,0:T(8,128)(2,1)S(1)}, u32[]{:S(2)}, u32[]{:S(2)}) collective-permute-start(bf16[256,256]{1,0:T(8,128)(2,1)S(1)} %copy-done.14), channel_id=1, source_target_pairs={{0,4},{1,5},{2,6},{3,7},{4,0},{5,1},{6,2},{7,3},{8,12},{9,13},{10,... | collective-permute-start | bytes 393224 | tf_op jit(solution)/shard_map/ppermute | solution.py:49
  17.2 21.3 %collective-permute-start.11 = (bf16[256,256]{1,0:T(8,128)(2,1)S(1)}, bf16[256,256]{1,0:T(8,128)(2,1)S(1)}, u32[]{:S(2)}, u32[]{:S(2)}) collective-permute-start(bf16[256,256]{1,0:T(8,128)(2,1)S(1)} %copy-done.14), channel_id=1, source_target_pairs={{0,2},{1,3},{2,0},{3,1},{4,6},{5,7},{6,4},{7,5},{8,10},{9,11},{10,... | collective-permute-start | bytes 393224 | tf_op jit(solution)/shard_map/ppermute | solution.py:49
  18.5 8.0 %collective-permute-start.3 = (bf16[1,32,2048]{2,1,0:T(8,128)(2,1)S(1)}, bf16[1,32,2048]{2,1,0:T(8,128)(2,1)S(1)}, u32[]{:S(2)}, u32[]{:S(2)}) collective-permute-start(bf16[1,32,2048]{2,1,0:T(8,128)(2,1)S(1)} %get-tuple-element.68), channel_id=1, source_target_pairs={{0,6},{1,7},{2,4},{3,5},{4,2},{5,3},{6,0},{7,1},{8,14},{9,15},{10,... | collective-permute-start | bytes 393224 | tf_op jit(solution)/shard_map/ppermute | solution.py:49
  22.9 6.2 %collective-permute-start.2 = (bf16[1,32,2048]{2,1,0:T(8,128)(2,1)S(1)}, bf16[1,32,2048]{2,1,0:T(8,128)(2,1)S(1)}, u32[]{:S(2)}, u32[]{:S(2)}) collective-permute-start(bf16[1,32,2048]{2,1,0:T(8,128)(2,1)S(1)} %get-tuple-element.69), channel_id=1, source_target_pairs={{0,4},{1,5},{2,6},{3,7},{4,0},{5,1},{6,2},{7,3},{8,12},{9,13},{10,... | collective-permute-start | bytes 393224 | tf_op jit(solution)/shard_map/ppermute | solution.py:49
  26.5 5.0 %collective-permute-start.1 = (bf16[1,32,2048]{2,1,0:T(8,128)(2,1)S(1)}, bf16[1,32,2048]{2,1,0:T(8,128)(2,1)S(1)}, u32[]{:S(2)}, u32[]{:S(2)}) collective-permute-start(bf16[1,32,2048]{2,1,0:T(8,128)(2,1)S(1)} %get-tuple-element.70), channel_id=1, source_target_pairs={{0,2},{1,3},{2,0},{3,1},{4,6},{5,7},{6,4},{7,5},{8,10},{9,11},{10,... | collective-permute-start | bytes 393224 | tf_op jit(solution)/shard_map/ppermute | solution.py:49
  35.1 9.2 %collective-permute-start.6 = (bf16[1,32,2176]{2,1,0:T(8,128)(2,1)}, bf16[1,32,2176]{2,1,0:T(8,128)(2,1)S(1)}, u32[]{:S(2)}, u32[]{:S(2)}) collective-permute-start(bf16[1,32,2176]{2,1,0:T(8,128)(2,1)} %get-tuple-element.35.refs_0_), channel_id=1, source_target_pairs={{0,6},{1,7},{2,4},{3,5},{4,2},{5,3},{6,0},{7,1},{8,14},{9,15},{10,... | collective-permute-start | bytes 417800 | tf_op jit(solution)/shard_map/ppermute | solution.py:49
  37.8 1.3 collective-permute-start.14
  37.8 1.8 %collective-permute-start.17 = (bf16[256,256]{1,0:T(8,128)(2,1)S(1)}, bf16[256,256]{1,0:T(8,128)(2,1)S(1)}, u32[]{:S(2)}, u32[]{:S(2)}) collective-permute-start(bf16[256,256]{1,0:T(8,128)(2,1)S(1)} %collective-permute-done.13.refs_3_), channel_id=1, source_target_pairs={{0,1},{1,0},{2,3},{3,2},{4,5},{5,4},{6,7},{7,6},{8,9},{9,8},{10,11... | collective-permute-start | bytes 393224 | tf_op jit(solution)/shard_map/ppermute | solution.py:49
  38.4 1.6 %collective-permute-start.16 = (bf16[256,256]{1,0:T(8,128)(2,1)S(1)}, bf16[256,256]{1,0:T(8,128)(2,1)S(1)}, u32[]{:S(2)}, u32[]{:S(2)}) collective-permute-start(bf16[256,256]{1,0:T(8,128)(2,1)S(1)} %collective-permute-done.12.refs_2_), channel_id=1, source_target_pairs={{0,1},{1,0},{2,3},{3,2},{4,5},{5,4},{6,7},{7,6},{8,9},{9,8},{10,11... | collective-permute-start | bytes 393224 | tf_op jit(solution)/shard_map/ppermute | solution.py:49
  38.4 3.3 %collective-permute-start.15 = (bf16[256,256]{1,0:T(8,128)(2,1)S(1)}, bf16[256,256]{1,0:T(8,128)(2,1)S(1)}, u32[]{:S(2)}, u32[]{:S(2)}) collective-permute-start(bf16[256,256]{1,0:T(8,128)(2,1)S(1)} %collective-permute-done.11.refs_1_), channel_id=1, source_target_pairs={{0,1},{1,0},{2,3},{3,2},{4,5},{5,4},{6,7},{7,6},{8,9},{9,8},{10,11... | collective-permute-start | bytes 393224 | tf_op jit(solution)/shard_map/ppermute | solution.py:49
  39.2 13.7 %collective-permute-start.5 = (bf16[1,32,2176]{2,1,0:T(8,128)(2,1)}, bf16[1,32,2176]{2,1,0:T(8,128)(2,1)S(1)}, u32[]{:S(2)}, u32[]{:S(2)}) collective-permute-start(bf16[1,32,2176]{2,1,0:T(8,128)(2,1)} %get-tuple-element.35.refs_0_), channel_id=1, source_target_pairs={{0,4},{1,5},{2,6},{3,7},{4,0},{5,1},{6,2},{7,3},{8,12},{9,13},{10,... | collective-permute-start | bytes 417800 | tf_op jit(solution)/shard_map/ppermute | solution.py:49
  39.7 13.3 %collective-permute-start.4 = (bf16[1,32,2176]{2,1,0:T(8,128)(2,1)}, bf16[1,32,2176]{2,1,0:T(8,128)(2,1)S(1)}, u32[]{:S(2)}, u32[]{:S(2)}) collective-permute-start(bf16[1,32,2176]{2,1,0:T(8,128)(2,1)} %get-tuple-element.35.refs_0_), channel_id=1, source_target_pairs={{0,2},{1,3},{2,0},{3,1},{4,6},{5,7},{6,4},{7,5},{8,10},{9,11},{10,... | collective-permute-start | bytes 417800 | tf_op jit(solution)/shard_map/ppermute | solution.py:49
  40.0 13.6 %collective-permute-start.21 = (bf16[32,2688]{1,0:T(8,128)(2,1)}, bf16[32,2688]{1,0:T(8,128)(2,1)S(1)}, u32[]{:S(2)}, u32[]{:S(2)}) collective-permute-start(bf16[32,2688]{1,0:T(8,128)(2,1)} %get-tuple-element.43), channel_id=1, source_target_pairs={{0,8},{8,0},{16,24},{24,16},{1,9},{9,1},{17,25},{25,17},{2,10},{10... | collective-permute-start | bytes 516104 | tf_op jit(solution)/shard_map/ppermute | solution.py:49
  41.8 15.7 %collective-permute-start.22 = (bf16[32,2688]{1,0:T(8,128)(2,1)}, bf16[32,2688]{1,0:T(8,128)(2,1)S(1)}, u32[]{:S(2)}, u32[]{:S(2)}) collective-permute-start(bf16[32,2688]{1,0:T(8,128)(2,1)} %get-tuple-element.44), channel_id=1, source_target_pairs={{0,16},{8,24},{16,0},{24,8},{1,17},{9,25},{17,1},{25,9},{2,18},{10... | collective-permute-start | bytes 516104 | tf_op jit(solution)/shard_map/ppermute | solution.py:49
  44.4 13.1 %collective-permute-start.23 = (bf16[32,2688]{1,0:T(8,128)(2,1)}, bf16[32,2688]{1,0:T(8,128)(2,1)S(1)}, u32[]{:S(2)}, u32[]{:S(2)}) collective-permute-start(bf16[32,2688]{1,0:T(8,128)(2,1)} %get-tuple-element.45), channel_id=1, source_target_pairs={{0,24},{8,16},{16,8},{24,0},{1,25},{9,17},{17,9},{25,1},{2,26},{10... | collective-permute-start | bytes 516104 | tf_op jit(solution)/shard_map/ppermute | solution.py:49
  52.9 30.7 %copy-start = (bf16[1024,256]{1,0:T(8,128)(2,1)S(1)}, bf16[1024,256]{1,0:T(8,128)(2,1)}, u32[]{:S(2)}) copy-start(bf16[1024,256]{1,0:T(8,128)(2,1)} %get-tuple-element.51.refs_0_) | copy-start | bytes 1572868
  52.9 7.2 %collective-permute-start.7 = (bf16[1,32,2176]{2,1,0:T(8,128)(2,1)S(1)}, bf16[1,32,2176]{2,1,0:T(8,128)(2,1)S(1)}, u32[]{:S(2)}, u32[]{:S(2)}) collective-permute-start(bf16[1,32,2176]{2,1,0:T(8,128)(2,1)S(1)} %copy-done.5), channel_id=1, source_target_pairs={{0,1},{1,0},{2,3},{3,2},{4,5},{5,4},{6,7},{7,6},{8,9},{9,8},{10,11... | collective-permute-start | bytes 417800 | tf_op jit(solution)/shard_map/ppermute | solution.py:49
  53.0 7.6 %collective-permute-start.10 = (bf16[1,32,2176]{2,1,0:T(8,128)(2,1)S(1)}, bf16[1,32,2176]{2,1,0:T(8,128)(2,1)S(1)}, u32[]{:S(2)}, u32[]{:S(2)}) collective-permute-start(bf16[1,32,2176]{2,1,0:T(8,128)(2,1)S(1)} %collective-permute-done.6.refs_3_), channel_id=1, source_target_pairs={{0,1},{1,0},{2,3},{3,2},{4,5},{5,4},{6,7},{7,6},{8,9},{9,8},{10,11... | collective-permute-start | bytes 417800 | tf_op jit(solution)/shard_map/ppermute | solution.py:49
  53.6 7.6 %collective-permute-start.9 = (bf16[1,32,2176]{2,1,0:T(8,128)(2,1)S(1)}, bf16[1,32,2176]{2,1,0:T(8,128)(2,1)S(1)}, u32[]{:S(2)}, u32[]{:S(2)}) collective-permute-start(bf16[1,32,2176]{2,1,0:T(8,128)(2,1)S(1)} %collective-permute-done.5.refs_2_), channel_id=1, source_target_pairs={{0,1},{1,0},{2,3},{3,2},{4,5},{5,4},{6,7},{7,6},{8,9},{9,8},{10,11... | collective-permute-start | bytes 417800 | tf_op jit(solution)/shard_map/ppermute | solution.py:49
  57.5 3.7 %collective-permute-start.8 = (bf16[1,32,2176]{2,1,0:T(8,128)(2,1)S(1)}, bf16[1,32,2176]{2,1,0:T(8,128)(2,1)S(1)}, u32[]{:S(2)}, u32[]{:S(2)}) collective-permute-start(bf16[1,32,2176]{2,1,0:T(8,128)(2,1)S(1)} %collective-permute-done.4.refs_1_), channel_id=1, source_target_pairs={{0,1},{1,0},{2,3},{3,2},{4,5},{5,4},{6,7},{7,6},{8,9},{9,8},{10,11... | collective-permute-start | bytes 417800 | tf_op jit(solution)/shard_map/ppermute | solution.py:49
  57.6 59.4 %copy-start.4 = (bf16[3,32,2688]{2,1,0:T(8,128)(2,1)}, bf16[3,32,2688]{2,1,0:T(8,128)(2,1)S(1)}, u32[]{:S(2)}) copy-start(bf16[3,32,2688]{2,1,0:T(8,128)(2,1)S(1)} %pad_maximum_fusion.refs_0_) | copy-start | bytes 1548292
  57.6 46.1 %collective-permute-start.26 = (bf16[3,32,2688]{2,1,0:T(8,128)(2,1)S(1)}, bf16[3,32,2688]{2,1,0:T(8,128)(2,1)S(1)}, u32[]{:S(2)}, u32[]{:S(2)}) collective-permute-start(bf16[3,32,2688]{2,1,0:T(8,128)(2,1)S(1)} %pad_maximum_fusion.refs_0_), channel_id=1, source_target_pairs={{0,6},{1,7},{2,4},{3,5},{4,2},{5,3},{6,0},{7,1},{8,14},{9,15},{10,... | collective-permute-start | bytes 1548296 | tf_op jit(solution)/shard_map/ppermute | solution.py:49
  60.2 44.1 %collective-permute-start.25 = (bf16[3,32,2688]{2,1,0:T(8,128)(2,1)S(1)}, bf16[3,32,2688]{2,1,0:T(8,128)(2,1)}, u32[]{:S(2)}, u32[]{:S(2)}) collective-permute-start(bf16[3,32,2688]{2,1,0:T(8,128)(2,1)S(1)} %pad_maximum_fusion.refs_0_), channel_id=1, source_target_pairs={{0,4},{1,5},{2,6},{3,7},{4,0},{5,1},{6,2},{7,3},{8,12},{9,13},{10,... | collective-permute-start | bytes 1548296 | tf_op jit(solution)/shard_map/ppermute | solution.py:49
  60.7 43.6 %collective-permute-start.24 = (bf16[3,32,2688]{2,1,0:T(8,128)(2,1)S(1)}, bf16[3,32,2688]{2,1,0:T(8,128)(2,1)}, u32[]{:S(2)}, u32[]{:S(2)}) collective-permute-start(bf16[3,32,2688]{2,1,0:T(8,128)(2,1)S(1)} %pad_maximum_fusion.refs_0_), channel_id=1, source_target_pairs={{0,2},{1,3},{2,0},{3,1},{4,6},{5,7},{6,4},{7,5},{8,10},{9,11},{10,... | collective-permute-start | bytes 1548296 | tf_op jit(solution)/shard_map/ppermute | solution.py:49
  65.4 5.9 %collective-permute-start.20 = (bf16[16,512]{1,0:T(8,128)(2,1)}, bf16[16,512]{1,0:T(8,128)(2,1)S(1)}, u32[]{:S(2)}, u32[]{:S(2)}) collective-permute-start(bf16[16,512]{1,0:T(8,128)(2,1)} %get-tuple-element.37.refs_0_), channel_id=1, source_target_pairs={{0,24},{8,16},{16,8},{24,0},{1,25},{9,17},{17,9},{25,1},{2,26},{10... | collective-permute-start | bytes 49160 | tf_op jit(solution)/shard_map/ppermute | solution.py:49
  67.8 5.1 %collective-permute-start.19 = (bf16[16,512]{1,0:T(8,128)(2,1)}, bf16[16,512]{1,0:T(8,128)(2,1)S(1)}, u32[]{:S(2)}, u32[]{:S(2)}) collective-permute-start(bf16[16,512]{1,0:T(8,128)(2,1)} %get-tuple-element.37.refs_0_), channel_id=1, source_target_pairs={{0,16},{8,24},{16,0},{24,8},{1,17},{9,25},{17,1},{25,9},{2,18},{10... | collective-permute-start | bytes 49160 | tf_op jit(solution)/shard_map/ppermute | solution.py:49
  71.3 3.9 %collective-permute-start.18 = (bf16[16,512]{1,0:T(8,128)(2,1)}, bf16[16,512]{1,0:T(8,128)(2,1)S(1)}, u32[]{:S(2)}, u32[]{:S(2)}) collective-permute-start(bf16[16,512]{1,0:T(8,128)(2,1)} %get-tuple-element.37.refs_0_), channel_id=1, source_target_pairs={{0,8},{8,0},{16,24},{24,16},{1,9},{9,1},{17,25},{25,17},{2,10},{10... | collective-permute-start | bytes 49160 | tf_op jit(solution)/shard_map/ppermute | solution.py:49
  79.5 4.1 %collective-permute-start.34 = (bf16[64,256]{1,0:T(8,128)(2,1)}, bf16[64,256]{1,0:T(8,128)(2,1)S(1)}, u32[]{:S(2)}, u32[]{:S(2)}) collective-permute-start(bf16[64,256]{1,0:T(8,128)(2,1)} %get-tuple-element.53), channel_id=1, source_target_pairs={{0,8},{8,0},{16,24},{24,16},{1,9},{9,1},{17,25},{25,17},{2,10},{10... | collective-permute-start | bytes 98312 | tf_op jit(solution)/shard_map/ppermute | solution.py:49
  80.4 17.3 %collective-permute-start.35 = (bf16[64,256]{1,0:T(8,128)(2,1)}, bf16[64,256]{1,0:T(8,128)(2,1)S(1)}, u32[]{:S(2)}, u32[]{:S(2)}) collective-permute-start(bf16[64,256]{1,0:T(8,128)(2,1)} %get-tuple-element.54), channel_id=1, source_target_pairs={{0,16},{8,24},{16,0},{24,8},{1,17},{9,25},{17,1},{25,9},{2,18},{10... | collective-permute-start | bytes 98312 | tf_op jit(solution)/shard_map/ppermute | solution.py:49
  83.6 21.9 %collective-permute-start.33 = (bf16[1024,256]{1,0:T(8,128)(2,1)S(1)}, bf16[1024,256]{1,0:T(8,128)(2,1)S(1)}, u32[]{:S(2)}, u32[]{:S(2)}) collective-permute-start(bf16[1024,256]{1,0:T(8,128)(2,1)S(1)} %copy-done), channel_id=1, source_target_pairs={{0,24},{8,16},{16,8},{24,0},{1,25},{9,17},{17,9},{25,1},{2,26},{10... | collective-permute-start | bytes 1572872 | tf_op jit(solution)/shard_map/ppermute | solution.py:49
  97.7 6.0 %collective-permute-start.36 = (bf16[64,256]{1,0:T(8,128)(2,1)}, bf16[64,256]{1,0:T(8,128)(2,1)S(1)}, u32[]{:S(2)}, u32[]{:S(2)}) collective-permute-start(bf16[64,256]{1,0:T(8,128)(2,1)} %get-tuple-element.55), channel_id=1, source_target_pairs={{0,24},{8,16},{16,8},{24,0},{1,25},{9,17},{17,9},{25,1},{2,26},{10... | collective-permute-start | bytes 98312 | tf_op jit(solution)/shard_map/ppermute | solution.py:49
  103.7 9.3 %collective-permute-start.27 = (bf16[3,32,2688]{2,1,0:T(8,128)(2,1)S(1)}, bf16[3,32,2688]{2,1,0:T(8,128)(2,1)}, u32[]{:S(2)}, u32[]{:S(2)}) collective-permute-start(bf16[3,32,2688]{2,1,0:T(8,128)(2,1)S(1)} %pad_maximum_fusion.refs_0_), channel_id=1, source_target_pairs={{0,1},{1,0},{2,3},{3,2},{4,5},{5,4},{6,7},{7,6},{8,9},{9,8},{10,11... | collective-permute-start | bytes 1548296 | tf_op jit(solution)/shard_map/ppermute | solution.py:49
  103.7 13.3 %copy-start.32 = (bf16[3,32,2688]{2,1,0:T(8,128)(2,1)}, bf16[3,32,2688]{2,1,0:T(8,128)(2,1)S(1)}, u32[]{:S(2)}) copy-start(bf16[3,32,2688]{2,1,0:T(8,128)(2,1)S(1)} %collective-permute-done.26.refs_3_) | copy-start | bytes 1548292
  103.7 9.3 %collective-permute-start.30 = (bf16[3,32,2688]{2,1,0:T(8,128)(2,1)S(1)}, bf16[3,32,2688]{2,1,0:T(8,128)(2,1)S(1)}, u32[]{:S(2)}, u32[]{:S(2)}) collective-permute-start(bf16[3,32,2688]{2,1,0:T(8,128)(2,1)S(1)} %collective-permute-done.26.refs_3_), channel_id=1, source_target_pairs={{0,1},{1,0},{2,3},{3,2},{4,5},{5,4},{6,7},{7,6},{8,9},{9,8},{10,11... | collective-permute-start | bytes 1548296 | tf_op jit(solution)/shard_map/ppermute | solution.py:49
  104.2 11.2 %collective-permute-start.29 = (bf16[3,32,2688]{2,1,0:T(8,128)(2,1)}, bf16[3,32,2688]{2,1,0:T(8,128)(2,1)S(1)}, u32[]{:S(2)}, u32[]{:S(2)}) collective-permute-start(bf16[3,32,2688]{2,1,0:T(8,128)(2,1)} %collective-permute-done.25.refs_2_), channel_id=1, source_target_pairs={{0,1},{1,0},{2,3},{3,2},{4,5},{5,4},{6,7},{7,6},{8,9},{9,8},{10,11... | collective-permute-start | bytes 1548296 | tf_op jit(solution)/shard_map/ppermute | solution.py:49
  104.3 11.8 %collective-permute-start.28 = (bf16[3,32,2688]{2,1,0:T(8,128)(2,1)}, bf16[3,32,2688]{2,1,0:T(8,128)(2,1)S(1)}, u32[]{:S(2)}, u32[]{:S(2)}) collective-permute-start(bf16[3,32,2688]{2,1,0:T(8,128)(2,1)} %collective-permute-done.24.refs_1_), channel_id=1, source_target_pairs={{0,1},{1,0},{2,3},{3,2},{4,5},{5,4},{6,7},{7,6},{8,9},{9,8},{10,11... | collective-permute-start | bytes 1548296 | tf_op jit(solution)/shard_map/ppermute | solution.py:49
  105.5 23.2 %copy-start.1 = (bf16[1024,256]{1,0:T(8,128)(2,1)}, bf16[1024,256]{1,0:T(8,128)(2,1)S(1)}, u32[]{:S(2)}) copy-start(bf16[1024,256]{1,0:T(8,128)(2,1)S(1)} %collective-permute-done.33.refs_3_) | copy-start | bytes 1572868
  105.5 2.3 %collective-permute-start.37 = (bf16[64,256]{1,0:T(8,128)(2,1)S(1)}, bf16[64,256]{1,0:T(8,128)(2,1)S(1)}, u32[]{:S(2)}, u32[]{:S(2)}) collective-permute-start(bf16[64,256]{1,0:T(8,128)(2,1)S(1)} %add_convert_fusion.4), channel_id=1, source_target_pairs={{0,1},{1,0},{2,3},{3,2},{4,5},{5,4},{6,7},{7,6},{8,9},{9,8},{10,11... | collective-permute-start | bytes 98312 | tf_op jit(solution)/shard_map/ppermute | solution.py:49
  107.8 28.6 %collective-permute-start.32 = (bf16[1024,256]{1,0:T(8,128)(2,1)S(1)}, bf16[1024,256]{1,0:T(8,128)(2,1)S(1)}, u32[]{:S(2)}, u32[]{:S(2)}) collective-permute-start(bf16[1024,256]{1,0:T(8,128)(2,1)S(1)} %copy-done), channel_id=1, source_target_pairs={{0,16},{8,24},{16,0},{24,8},{1,17},{9,25},{17,1},{25,9},{2,18},{10... | collective-permute-start | bytes 1572872 | tf_op jit(solution)/shard_map/ppermute | solution.py:49
  113.0 23.5 %collective-permute-start.31 = (bf16[1024,256]{1,0:T(8,128)(2,1)S(1)}, bf16[1024,256]{1,0:T(8,128)(2,1)S(1)}, u32[]{:S(2)}, u32[]{:S(2)}) collective-permute-start(bf16[1024,256]{1,0:T(8,128)(2,1)S(1)} %copy-done), channel_id=1, source_target_pairs={{0,8},{8,0},{16,24},{24,16},{1,9},{9,1},{17,25},{25,17},{2,10},{10... | collective-permute-start | bytes 1572872 | tf_op jit(solution)/shard_map/ppermute | solution.py:49
  113.0 15.7 %copy-start.13 = (bf16[64,256]{1,0:T(8,128)(2,1)}, bf16[64,256]{1,0:T(8,128)(2,1)S(1)}, u32[]{:S(2)}) copy-start(bf16[64,256]{1,0:T(8,128)(2,1)S(1)} %add_convert_fusion.3.refs_4_) | copy-start | bytes 98308
  113.0 23.4 %collective-permute-start.40 = (bf16[64,256]{1,0:T(8,128)(2,1)S(1)}, bf16[64,256]{1,0:T(8,128)(2,1)S(1)}, u32[]{:S(2)}, u32[]{:S(2)}) collective-permute-start(bf16[64,256]{1,0:T(8,128)(2,1)S(1)} %add_convert_fusion.3.refs_4_), channel_id=1, source_target_pairs={{0,6},{1,7},{2,4},{3,5},{4,2},{5,3},{6,0},{7,1},{8,14},{9,15},{10,... | collective-permute-start | bytes 98312 | tf_op jit(solution)/shard_map/ppermute | solution.py:49
  115.4 21.1 %collective-permute-start.39 = (bf16[64,256]{1,0:T(8,128)(2,1)S(1)}, bf16[64,256]{1,0:T(8,128)(2,1)S(1)}, u32[]{:S(2)}, u32[]{:S(2)}) collective-permute-start(bf16[64,256]{1,0:T(8,128)(2,1)S(1)} %add_convert_fusion.3.refs_4_), channel_id=1, source_target_pairs={{0,4},{1,5},{2,6},{3,7},{4,0},{5,1},{6,2},{7,3},{8,12},{9,13},{10,... | collective-permute-start | bytes 98312 | tf_op jit(solution)/shard_map/ppermute | solution.py:49
  116.2 20.3 %collective-permute-start.38 = (bf16[64,256]{1,0:T(8,128)(2,1)S(1)}, bf16[64,256]{1,0:T(8,128)(2,1)S(1)}, u32[]{:S(2)}, u32[]{:S(2)}) collective-permute-start(bf16[64,256]{1,0:T(8,128)(2,1)S(1)} %add_convert_fusion.3.refs_4_), channel_id=1, source_target_pairs={{0,2},{1,3},{2,0},{3,1},{4,6},{5,7},{6,4},{7,5},{8,10},{9,11},{10,... | collective-permute-start | bytes 98312 | tf_op jit(solution)/shard_map/ppermute | solution.py:49
  (30 other events, 117.1 us)
